TPU v7x, 128 devices: a whole 4x4x4 slice. The times are simulated.
128 devices in a mesh: row: 8 (over x, core), col: 16 (over y, z).
Axes of the slice: x: 4, y: 4, z: 4, core: 2. Of those that a mesh axis runs over, the one named last changes fastest.
Arguments:
- front_blocks: float32 [16, 1024, 8, 2048], P(None, 'row', None, 'col'), may hold values from -2.5 to 10.5, as said below
- child_updates: bfloat16 [2, 12, 1024, 6, 2048], P(None, None, 'row', None, 'col'), may hold values from -0.2 to 2.2, as said below
- child_map: int32 [2, 96], replicated, may hold values from 0 to 127, as said below
Outputs:
- factored: float32 [16, 1024, 8, 2048], P(None, 'row', None, 'col')
Inputs may be any that keep to these rules, and one draw needn't show every extreme that they name: `child_map`: for each child, block a * 16 + j (0 <= j < 16) lands in front block h_a * 16 + ((s_a - j) mod 16), with 6 distinct h_a below 8 and s_a = (s + q_a) mod 16, q a permutation of 0 .. 5. Hence along col one device sends at most 1 of a child's column blocks to one device, along row at most 2 of its row blocks, and both bounds are reached in every draw. `front_blocks`: symmetric positive definite. `child_updates`: each child update is symmetric.
All inputs are finite; a program needn't handle non-finite values.
Results may differ from a plain program's by a relative error of at most 0.0003.
Values may be sent and summed in bfloat16 or wider, within the bound.
A program may use at most 192 MiB of HBM per device.

v0:
```python
import jax
import jax.numpy as jnp
from jax import lax
from jax.sharding import PartitionSpec as P

PW = 256
PANELS = 2
PD = 512


def spread_2(value, axis, source):
    kept = jnp.where(lax.axis_index(axis) == source, value, 0).astype(value.dtype)
    return lax.psum(kept, axis)


def earlier_count(targets):
    count_all = targets.shape[1]
    matches = targets[:, :, None, :] == targets[:, None, :, :]
    order_ids = jnp.arange(count_all)
    before = (order_ids[None, :] < order_ids[:, None])[None, :, :, None]
    return jnp.sum(matches & before, axis=2)


def arrival_info(block_map, my_index, devices):
    child_count = block_map.shape[0]
    slot_total = block_map.shape[1] // devices
    block_grid = block_map.reshape(child_count, slot_total, devices)
    targets = block_grid % devices
    home_slots = block_grid // devices
    arriving = targets == my_index
    arrival_flat = arriving.reshape(child_count, slot_total * devices).astype(jnp.int32)
    positions = (jnp.cumsum(arrival_flat, axis=1) - 1).reshape(child_count, slot_total, devices)
    return (targets, home_slots, arriving, positions)


def route_tables(block_map, my_index, devices, capacity, slot_count):
    child_count = block_map.shape[0]
    slot_total = block_map.shape[1] // devices
    targets, home_slots, arriving, positions = arrival_info(block_map, my_index, devices)
    slot_ranks = earlier_count(targets)
    my_targets = lax.dynamic_index_in_dim(targets, my_index, axis=2, keepdims=False)
    my_ranks = lax.dynamic_index_in_dim(slot_ranks, my_index, axis=2, keepdims=False)
    child_ids = jnp.arange(child_count)[:, None]
    slot_values = jnp.broadcast_to(
        jnp.arange(slot_total, dtype=jnp.int32)[None, :], (child_count, slot_total)
    )
    send_index = jnp.full((child_count, devices * capacity), slot_total, jnp.int32)
    send_index = send_index.at[child_ids, my_targets * capacity + my_ranks].set(slot_values)
    sources = jnp.arange(devices, dtype=jnp.int32)[None, None, :]
    where_from = jnp.where(arriving, sources * capacity + slot_ranks, devices * capacity)
    where_to = jnp.where(arriving, home_slots, slot_count)
    place_index = jnp.full((child_count, slot_count + 1), devices * capacity, jnp.int32)
    place_index = place_index.at[child_ids[:, :, None], where_to].set(where_from)
    return (send_index, place_index[:, :slot_count])


def pick_slots(payload, index_table, axis_no):
    return jax.vmap(lambda part_data, part_index: jnp.take(part_data, part_index, axis=axis_no))(
        payload, index_table
    )


def move_rows(payload, block_map, slot_count):
    devices = lax.axis_size("row")
    my_index = lax.axis_index("row")
    col_devices = lax.axis_size("col")
    child_count, slot_total, tile_size, row_width = payload.shape
    col_slots = block_map.shape[1] // col_devices
    capacity = col_devices // devices * ((col_slots + devices - 1) // devices)
    send_index, place_index = route_tables(block_map, my_index, devices, capacity, slot_count)
    padded = jnp.concatenate(
        [payload, jnp.zeros((child_count, 1, tile_size, row_width), payload.dtype)], axis=1
    )
    outgoing = pick_slots(padded, send_index, 0).reshape(
        child_count, devices * capacity * tile_size, row_width
    )
    incoming = lax.all_to_all(outgoing, "row", split_axis=1, concat_axis=1, tiled=True)
    incoming = incoming.reshape(child_count, devices * capacity, tile_size, row_width)
    padded_in = jnp.concatenate(
        [incoming, jnp.zeros((child_count, 1, tile_size, row_width), incoming.dtype)], axis=1
    )
    return pick_slots(padded_in, place_index, 0)


def move_columns(payload, block_map, slot_count):
    devices = lax.axis_size("col")
    my_index = lax.axis_index("col")
    child_count, height, slot_total, tile_size = payload.shape
    capacity = (slot_total + devices - 1) // devices
    send_index, place_index = route_tables(block_map, my_index, devices, capacity, slot_count)
    padded = jnp.concatenate(
        [payload, jnp.zeros((child_count, height, 1, tile_size), payload.dtype)], axis=2
    )
    outgoing = pick_slots(padded, send_index, 1).reshape(
        child_count, height, devices * capacity * tile_size
    )
    incoming = lax.all_to_all(outgoing, "col", split_axis=2, concat_axis=2, tiled=True)
    incoming = incoming.reshape(child_count, height, devices * capacity, tile_size)
    padded_in = jnp.concatenate(
        [incoming, jnp.zeros((child_count, height, 1, tile_size), incoming.dtype)], axis=2
    )
    return pick_slots(padded_in, place_index, 1)


def on_device(front_blocks, child_updates, child_map):
    row_count = lax.axis_size("row")
    col_count = lax.axis_size("col")
    row_index = lax.axis_index("row")
    col_index = lax.axis_index("col")
    front_slots_r = front_blocks.shape[0]
    tile_size = front_blocks.shape[1]
    front_slots_c = front_blocks.shape[2]
    child_count = child_updates.shape[0]
    child_rows = child_updates.shape[1]
    child_cols = child_updates.shape[3]
    arrived = move_rows(
        child_updates.reshape(child_count, child_rows, tile_size, child_cols * tile_size),
        child_map,
        front_slots_r,
    )
    arrived = move_columns(
        arrived.reshape(child_count, front_slots_r * tile_size, child_cols, tile_size),
        child_map,
        front_slots_c,
    )
    height = front_slots_r * tile_size
    breadth = front_slots_c * tile_size
    children_sum = jnp.sum(arrived.astype(jnp.float32), axis=0).reshape(height, breadth)
    assembled = front_blocks.reshape(height, breadth) + children_sum
    local_rows = jnp.arange(height, dtype=jnp.int32)
    row_global = (
        local_rows // tile_size * row_count + row_index
    ) * tile_size + local_rows % tile_size
    local_cols = jnp.arange(breadth, dtype=jnp.int32)
    col_global = (
        local_cols // tile_size * col_count + col_index
    ) * tile_size + local_cols % tile_size
    panel_tiles = PW // tile_size
    spread = col_count // row_count
    row_factors = []
    col_factors = []
    for panel_no in range(PANELS):
        first_col = panel_no * PW
        finish = first_col + PW
        column_tiles = []
        for tile_no in range(panel_tiles):
            global_tile = panel_no * panel_tiles + tile_no
            col_slot = global_tile // col_count
            column_tile = assembled[:, col_slot * tile_size : (col_slot + 1) * tile_size]
            column_tiles.append(column_tile)
        pieces = [
            jnp.where(
                col_index == (panel_no * panel_tiles + tile_no) % col_count,
                column_tiles[tile_no],
                0.0,
            )
            for tile_no in range(panel_tiles)
        ]
        panel_rows = lax.psum(jnp.concatenate(pieces, axis=1), "col")
        diag_pieces = []
        for tile_no in range(panel_tiles):
            global_tile = panel_no * panel_tiles + tile_no
            row_slot = global_tile // row_count
            diag_pieces.append(
                jnp.where(
                    row_index == global_tile % row_count,
                    panel_rows[row_slot * tile_size : (row_slot + 1) * tile_size],
                    0.0,
                )
            )
        diagonal = lax.psum(jnp.concatenate(diag_pieces, axis=0), "row")
        factor = jnp.linalg.cholesky(diagonal)
        solved = lax.linalg.triangular_solve(
            factor, panel_rows, left_side=False, lower=True, transpose_a=True
        )
        lower_part = jnp.where(row_global[:, None] >= finish, solved, 0.0)
        inside = (row_global >= first_col) & (row_global < finish)
        factor_rows = jnp.take(factor, jnp.clip(row_global - first_col, 0, PW - 1), axis=0)
        lower_part = jnp.where(inside[:, None], factor_rows, lower_part)
        chosen = lax.dynamic_index_in_dim(
            lower_part.reshape(front_slots_c, spread, tile_size, PW),
            col_index // row_count,
            axis=1,
            keepdims=False,
        ).reshape(breadth, PW)
        col_part = spread_2(chosen, "row", col_index % row_count)
        assembled = assembled - jnp.dot(
            lower_part,
            col_part.T,
            precision=lax.Precision.HIGHEST,
            preferred_element_type=jnp.float32,
        )
        row_factors.append(lower_part)
        col_factors.append(col_part)
    result = assembled
    for panel_no in range(PANELS):
        for tile_no in range(panel_tiles):
            global_tile = panel_no * panel_tiles + tile_no
            col_slot = global_tile // col_count
            owner_here = col_index == global_tile % col_count
            current = result[:, col_slot * tile_size : (col_slot + 1) * tile_size]
            fresh = row_factors[panel_no][:, tile_no * tile_size : (tile_no + 1) * tile_size]
            result = result.at[:, col_slot * tile_size : (col_slot + 1) * tile_size].set(
                jnp.where(owner_here, fresh, current)
            )
    upper_mask = (row_global[:, None] < PD) & (col_global[None, :] >= PD)
    result = jnp.where(upper_mask, 0.0, result)
    return result.reshape(front_slots_r, tile_size, front_slots_c, tile_size)


def solution(mesh):
    placed = (P(None, "row", None, "col"), P(None, None, "row", None, "col"), P())
    return jax.shard_map(
        on_device,
        mesh=mesh,
        in_specs=placed,
        out_specs=P(None, "row", None, "col"),
        check_vma=False,
    )
```

profile of v0, /device:TPU:0, one launch (start us, length us, event | category | flops | bytes accessed | tf_op | source)
XLA Modules:
  0.0 1366.0 jit_solution(4621265916315295728)
XLA Ops:
  54.3 44.7 %copy.74 = bf16[2,2048,768]{2,0,1:T(2,128)(2,1)} copy(bf16[2,2048,768]{2,1,0:T(8,128)(2,1)S(1)} %bitcast_select_fusion.1) | data formatting | bytes 12582912 | tf_op jit(solution)/shard_map/vmap(jit(_take))/select_n | solution.py:58
  104.3 71.8 %all-to-all-done = bf16[2,2048,768]{2,0,1:T(2,128)(2,1)} async-done(((bf16[2,2048,768]{2,0,1:T(2,128)(2,1)}), bf16[2,2048,768]{2,0,1:T(2,128)(2,1)}, u32[]{:S(2)}, u32[]{:S(2)}) %all-to-all-start) | async-done | bytes 6291488 | tf_op jit(solution)/shard_map/all_to_all | solution.py:77
  190.0 13.6 reshape.731
  222.9 22.5 %copy.78 = bf16[2,2048,16,128]{1,3,2,0:T(8,128)(2,1)} copy(bf16[2,2048,16,128]{3,1,2,0:T(8,128)(2,1)} %bitcast.147) | data formatting | bytes 33554432 | tf_op jit(solution)/shard_map/vmap(jit(_take))/gather | solution.py:58
  253.9 48.9 %copy.79 = bf16[2,2048,2048]{1,0,2:T(2,128)(2,1)} copy(bf16[2,2048,2048]{1,2,0:T(8,128)(2,1)S(1)} %bitcast_select_fusion) | data formatting | bytes 33554432 | tf_op jit(solution)/shard_map/vmap(jit(_take))/select_n | solution.py:58
  339.1 263.8 %all-to-all-done.1 = bf16[2,2048,2048]{1,0,2:T(2,128)(2,1)} async-done(((bf16[2,2048,2048]{1,0,2:T(2,128)(2,1)}), bf16[2,2048,2048]{1,0,2:T(2,128)(2,1)}, u32[]{:S(2)}, u32[]{:S(2)}) %all-to-all-start.1) | async-done | bytes 16777248 | tf_op jit(solution)/shard_map/all_to_all | solution.py:97
  602.9 41.1 %copy.81 = bf16[2,2048,16,128]{3,1,2,0:T(8,128)(2,1)} copy(bf16[2,2048,16,128]{1,0,3,2:T(2,128)(2,1)} %bitcast.9) | data formatting | bytes 33554432 | tf_op jit(solution)/shard_map/reshape | solution.py:98
  644.0 15.5 %concatenate.54 = bf16[2,2048,17,128]{3,1,2,0:T(8,128)(2,1)} pad(bf16[2,2048,16,128]{3,1,2,0:T(8,128)(2,1)} %copy.81, bf16[]{:T(256)} %constant.419.clone.1), padding=0_0x0_0x0_1x0_0 | pad | bytes 34603008 | tf_op jit(solution)/shard_map/concatenate | solution.py:99
  659.5 11.1 gather_fusion.3
  689.5 11.7 bitcast_add_fusion
  704.3 94.6 %all-reduce.12.cloned.1.call-done = f32[2048,256]{0,1:T(8,128)} async-done(((f32[2048,256]{0,1:T(8,128)}), f32[2048,256]{0,1:T(8,128)}) %all-reduce.12.cloned.1.call-update) | async-done | bytes 2097168 | tf_op jit(solution)/shard_map/psum | solution.py:159
  801.1 59.3 %all-reduce.14.cloned.1.call-done = f32[256,256]{0,1:T(8,128)} async-done(((f32[256,256]{0,1:T(8,128)}), f32[256,256]{0,1:T(8,128)}) %all-reduce.14.cloned.1.call-update) | async-done | bytes 262160 | tf_op jit(solution)/shard_map/psum | solution.py:171
  862.5 11.7 cholesky.130
  884.5 11.7 cholesky.147
  911.5 19.7 %custom-call.30 = f32[2,128,128]{1,2,0:T(8,128)S(1)} custom-call(f32[2,128,128]{2,1,0:T(8,128)S(1)} %get-tuple-element.70), custom_call_target="InvertDiagBlocksLowerTriangular" | custom-call | tf_op jit(solution)/shard_map/triangular_solve/custom-call.0 | solution.py:173
  946.2 61.6 %all-reduce.16.cloned.1.call-done = f32[1024,256]{0,1:T(8,128)} async-done(((f32[1024,256]{0,1:T(8,128)}), f32[1024,256]{0,1:T(8,128)}) %all-reduce.16.cloned.1.call-update) | async-done | bytes 1048592 | tf_op jit(solution)/shard_map/psum | solution.py:13
  1007.7 10.8 convolution_subtract_fusion.1
  1023.7 89.8 %all-reduce.18.cloned.1.call-done = f32[2048,256]{0,1:T(8,128)} async-done(((f32[2048,256]{0,1:T(8,128)}), f32[2048,256]{0,1:T(8,128)}) %all-reduce.18.cloned.1.call-update) | async-done | bytes 2097168 | tf_op jit(solution)/shard_map/psum | solution.py:159
  1115.3 59.6 %all-reduce.20.cloned.1.call-done = f32[256,256]{0,1:T(8,128)} async-done(((f32[256,256]{0,1:T(8,128)}), f32[256,256]{0,1:T(8,128)}) %all-reduce.20.cloned.1.call-update) | async-done | bytes 262160 | tf_op jit(solution)/shard_map/psum | solution.py:171
  1176.9 11.7 cholesky.164
  1199.0 11.7 cholesky.181
  1228.9 19.7 %custom-call.32 = f32[2,128,128]{1,2,0:T(8,128)S(1)} custom-call(f32[2,128,128]{2,1,0:T(8,128)S(1)} %get-tuple-element.71), custom_call_target="InvertDiagBlocksLowerTriangular" | custom-call | tf_op jit(solution)/shard_map/triangular_solve/custom-call.0 | solution.py:173
  1266.8 60.9 %all-reduce.22.cloned.1.call-done = f32[1024,256]{0,1:T(8,128)} async-done(((f32[1024,256]{0,1:T(8,128)}), f32[1024,256]{0,1:T(8,128)}) %all-reduce.22.cloned.1.call-update) | async-done | bytes 1048592 | tf_op jit(solution)/shard_map/psum | solution.py:13
  1327.7 10.8 convolution_subtract_fusion
  (177 shorter events, 278.7 us)
Async XLA Ops:
  99.0 77.1 %all-to-all-start = ((bf16[2,2048,768]{2,0,1:T(2,128)(2,1)}), bf16[2,2048,768]{2,0,1:T(2,128)(2,1)}, u32[]{:S(2)}, u32[]{:S(2)}) async-start(bf16[2,2048,768]{2,0,1:T(2,128)(2,1)} %copy.74), calls=%async_computation | async-start | bytes 12582912 | tf_op jit(solution)/shard_map/all_to_all | solution.py:77
  302.8 8.6 copy-start.4
  302.8 300.2 %all-to-all-start.1 = ((bf16[2,2048,2048]{1,0,2:T(2,128)(2,1)}), bf16[2,2048,2048]{1,0,2:T(2,128)(2,1)}, u32[]{:S(2)}, u32[]{:S(2)}) async-start(bf16[2,2048,2048]{1,0,2:T(2,128)(2,1)} %copy.79), calls=%async_computation.1 | async-start | bytes 33554432 | tf_op jit(solution)/shard_map/all_to_all | solution.py:97
  311.1 487.8 %all-reduce.12.cloned.1.call-start = ((), (), s32[]{:S(2)}) async-start(), calls=%async_computation.2 | async-start | bytes 4194304 | tf_op jit(solution)/shard_map/psum | solution.py:159
  704.2 156.2 %all-reduce.14.cloned.1.call-start = ((), (), s32[]{:S(2)}) async-start(), calls=%async_computation.3 | async-start | bytes 524288 | tf_op jit(solution)/shard_map/psum | solution.py:171
  800.6 207.2 %all-reduce.16.cloned.1.call-start = ((), (), s32[]{:S(2)}) async-start(), calls=%async_computation.4 | async-start | bytes 2097152 | tf_op jit(solution)/shard_map/psum | solution.py:13
  931.2 5.8 copy-start.3
  946.1 167.4 %all-reduce.18.cloned.1.call-start = ((), (), s32[]{:S(2)}) async-start(), calls=%async_computation.5 | async-start | bytes 4194304 | tf_op jit(solution)/shard_map/psum | solution.py:159
  1018.5 3.4 copy-start
  1023.7 151.2 %all-reduce.20.cloned.1.call-start = ((), (), s32[]{:S(2)}) async-start(), calls=%async_computation.6 | async-start | bytes 524288 | tf_op jit(solution)/shard_map/psum | solution.py:171
  1115.2 212.5 %all-reduce.22.cloned.1.call-start = ((), (), s32[]{:S(2)}) async-start(), calls=%async_computation.7 | async-start | bytes 2097152 | tf_op jit(solution)/shard_map/psum | solution.py:13
  1248.6 5.8 copy-start.2
  1338.5 2.0 copy-start.1
Sparse Core Ops, SparseCore 0:
  704.3 94.5 all-reduce.11
  801.3 58.9 all-reduce.13
  946.2 61.4 all-reduce.15
  1023.8 89.7 all-reduce.17
  1115.8 58.9 all-reduce.19
  1266.2 61.4 all-reduce.21
where the time goes:
time: 1380 us; the launch traced here: 1370 us
  waiting for transfers between devices  761 us (55%)
  local copies, waits for them, and re-layouts  364 us (26%)
  other arithmetic  176 us (13%)
  matrix products  34.1 us (2%)
  between operations  16.9 us (1%)
  starting transfers between devices  14.1 us (1%)
    all_to_all x1, waiting for transfers between devices, move_columns(): lax.all_to_all(outgoing, 'col', split_axis=2, concat_axis=2, tiled=True)  264 us
    psum x2, waiting for transfers between devices, on_device(): panel_rows = lax.psum(jnp.concatenate(pieces, axis=1), 'col')  184 us
    psum x2, waiting for transfers between devices, spread_2(): return lax.psum(kept, axis)  122 us
    psum x2, waiting for transfers between devices, on_device(): diagonal = lax.psum(jnp.concatenate(diag_pieces, axis=0), 'row')  119 us
    select_n x2, local copies, waits for them, and re-layouts, pick_slots(): jnp.take(part_data, part_index, axis=axis_no)  93.5 us
    gather x11, local copies, waits for them, and re-layouts, pick_slots(): jnp.take(part_data, part_index, axis=axis_no)  79.5 us
    all_to_all x1, waiting for transfers between devices, move_rows(): lax.all_to_all(outgoing, 'row', split_axis=1, concat_axis=1, tiled=True)  71.8 us
    another operation x14, other arithmetic, on_device(): factor = jnp.linalg.cholesky(diagonal)  69.2 us
  transfers between devices with their start and end apart: 8, of which 8 were waited for; matrix products, arithmetic and copies ran while one was open for 2% of the time, Pallas kernels for 0%

commit v1 on v0

--- a/solution.py
+++ b/solution.py
@@ -94,7 +94,10 @@
     outgoing = pick_slots(padded, send_index, 1).reshape(
         child_count, height, devices * capacity * tile_size
     )
-    incoming = lax.all_to_all(outgoing, "col", split_axis=2, concat_axis=2, tiled=True)
+    incoming = jnp.concatenate(
+        lax.all_to_all(jnp.stack(jnp.split(outgoing, lax.axis_size("col"), axis=2)), "col", 0, 0),
+        axis=2,
+    )
     incoming = incoming.reshape(child_count, height, devices * capacity, tile_size)
     padded_in = jnp.concatenate(
         [incoming, jnp.zeros((child_count, height, 1, tile_size), incoming.dtype)], axis=2

time: 1380 us -> 1290 us (0.935)
  local copies, waits for them, and re-layouts: 364 us -> 281 us
    select_n x2 -> x1, local copies, waits for them, and re-layouts: 93.5 us -> 44.7 us  [pick_slots(): jnp.take(part_data, part_index, axis=axis_no)]
    reshape x1 -> x0, local copies, waits for them, and re-layouts: 41.1 us -> none  [move_columns(): incoming.reshape(child_count, height, devices * capacity, tile_size)]
    unnamed x21 -> x36, local copies, waits for them, and re-layouts: 26.7 us -> 42.8 us
where the time goes in v1:
time: 1290 us; the launch traced here: 1280 us
  waiting for transfers between devices  761 us (59%)
  local copies, waits for them, and re-layouts  281 us (22%)
  other arithmetic  176 us (14%)
  matrix products  34.2 us (3%)
  between operations  16.8 us (1%)
  starting transfers between devices  14.1 us (1%)
    all_to_all x1, waiting for transfers between devices, move_columns(): lax.all_to_all(jnp.stack(jnp.split(outgoing, lax.axis_size('col'), axis=2...  264 us
    psum x2, waiting for transfers between devices, on_device(): panel_rows = lax.psum(jnp.concatenate(pieces, axis=1), 'col')  184 us
    psum x2, waiting for transfers between devices, spread_2(): return lax.psum(kept, axis)  122 us
    psum x2, waiting for transfers between devices, on_device(): diagonal = lax.psum(jnp.concatenate(diag_pieces, axis=0), 'row')  119 us
    gather x11, local copies, waits for them, and re-layouts, pick_slots(): jnp.take(part_data, part_index, axis=axis_no)  79.5 us
    all_to_all x1, waiting for transfers between devices, move_rows(): lax.all_to_all(outgoing, 'row', split_axis=1, concat_axis=1, tiled=True)  71.8 us
    another operation x14, other arithmetic, on_device(): factor = jnp.linalg.cholesky(diagonal)  69.2 us
    select_n x1, local copies, waits for them, and re-layouts, pick_slots(): jnp.take(part_data, part_index, axis=axis_no)  44.7 us
  transfers between devices with their start and end apart: 8, of which 8 were waited for; matrix products, arithmetic and copies ran while one was open for 2% of the time, Pallas kernels for 0%

profile of v1, /device:TPU:0, one launch (start us, length us, event | category | flops | bytes accessed | tf_op | source)
XLA Modules:
  0.0 1283.4 jit_solution(4071171554578456056)
XLA Ops:
  54.3 44.7 %copy.69 = bf16[2,2048,768]{2,0,1:T(2,128)(2,1)} copy(bf16[2,2048,768]{2,1,0:T(8,128)(2,1)S(1)} %bitcast_select_fusion.1) | data formatting | bytes 12582912 | tf_op jit(solution)/shard_map/vmap(jit(_take))/select_n | solution.py:58
  104.3 71.8 %all-to-all-done = bf16[2,2048,768]{2,0,1:T(2,128)(2,1)} async-done(((bf16[2,2048,768]{2,0,1:T(2,128)(2,1)}), bf16[2,2048,768]{2,0,1:T(2,128)(2,1)}, u32[]{:S(2)}, u32[]{:S(2)}) %all-to-all-start) | async-done | bytes 6291488 | tf_op jit(solution)/shard_map/all_to_all | solution.py:77
  190.0 13.6 %reshape.731 = bf16[2,2048,6,128]{3,2,1,0:T(8,128)(2,1)} reshape(bf16[32,128,768]{2,1,0:T(8,128)(2,1)} %gather_fusion.1) | data formatting | bytes 12582912 | tf_op jit(solution)/shard_map/vmap(jit(_take))/gather | solution.py:58
  212.6 10.3 gather_fusion.2
  222.9 22.5 %copy.73 = bf16[2,2048,16,128]{1,3,2,0:T(8,128)(2,1)} copy(bf16[2,2048,16,128]{3,1,2,0:T(8,128)(2,1)} %bitcast.212) | data formatting | bytes 33554432 | tf_op jit(solution)/shard_map/vmap(jit(_take))/gather | solution.py:58
  307.3 263.8 %all-to-all-done.1 = bf16[16,2,2048,128]{2,3,1,0:T(8,128)(2,1)} async-done(((bf16[16,2,2048,128]{2,3,1,0:T(8,128)(2,1)}), bf16[16,2,2048,128]{2,3,1,0:T(8,128)(2,1)}, u32[]{:S(2)}, u32[]{:S(2)}) %all-to-all-start.1) | async-done | bytes 16777248 | tf_op jit(solution)/shard_map/all_to_all | solution.py:98
  571.2 14.5 %concatenate.54 = bf16[2,2048,17,128]{1,3,0,2:T(8,128)(2,1)} pad(bf16[2,2048,16,128]{1,3,0,2:T(8,128)(2,1)} %bitcast.25, bf16[]{:T(256)} %constant.419.clone.1), padding=0_0x0_0x0_1x0_0 | pad | bytes 34603008 | tf_op jit(solution)/shard_map/concatenate | solution.py:102
  585.7 11.1 gather_fusion.3
  606.5 11.9 bitcast_add_fusion
  621.4 94.6 %all-reduce.12.cloned.1.call-done = f32[2048,256]{0,1:T(8,128)} async-done(((f32[2048,256]{0,1:T(8,128)}), f32[2048,256]{0,1:T(8,128)}) %all-reduce.12.cloned.1.call-update) | async-done | bytes 2097168 | tf_op jit(solution)/shard_map/psum | solution.py:162
  718.2 59.3 %all-reduce.14.cloned.1.call-done = f32[256,256]{0,1:T(8,128)} async-done(((f32[256,256]{0,1:T(8,128)}), f32[256,256]{0,1:T(8,128)}) %all-reduce.14.cloned.1.call-update) | async-done | bytes 262160 | tf_op jit(solution)/shard_map/psum | solution.py:174
  779.5 11.7 cholesky.130
  801.6 11.7 cholesky.147
  828.8 19.7 %custom-call.30 = f32[2,128,128]{1,2,0:T(8,128)S(1)} custom-call(f32[2,128,128]{2,1,0:T(8,128)S(1)} %get-tuple-element.70), custom_call_target="InvertDiagBlocksLowerTriangular" | custom-call | tf_op jit(solution)/shard_map/triangular_solve/custom-call.0 | solution.py:176
  863.6 61.6 %all-reduce.16.cloned.1.call-done = f32[1024,256]{0,1:T(8,128)} async-done(((f32[1024,256]{0,1:T(8,128)}), f32[1024,256]{0,1:T(8,128)}) %all-reduce.16.cloned.1.call-update) | async-done | bytes 1048592 | tf_op jit(solution)/shard_map/psum | solution.py:13
  925.1 10.8 convolution_subtract_fusion.1
  941.1 89.8 %all-reduce.18.cloned.1.call-done = f32[2048,256]{0,1:T(8,128)} async-done(((f32[2048,256]{0,1:T(8,128)}), f32[2048,256]{0,1:T(8,128)}) %all-reduce.18.cloned.1.call-update) | async-done | bytes 2097168 | tf_op jit(solution)/shard_map/psum | solution.py:162
  1032.7 59.6 %all-reduce.20.cloned.1.call-done = f32[256,256]{0,1:T(8,128)} async-done(((f32[256,256]{0,1:T(8,128)}), f32[256,256]{0,1:T(8,128)}) %all-reduce.20.cloned.1.call-update) | async-done | bytes 262160 | tf_op jit(solution)/shard_map/psum | solution.py:174
  1094.4 11.7 cholesky.164
  1116.4 11.7 cholesky.181
  1146.3 19.7 %custom-call.32 = f32[2,128,128]{1,2,0:T(8,128)S(1)} custom-call(f32[2,128,128]{2,1,0:T(8,128)S(1)} %get-tuple-element.71), custom_call_target="InvertDiagBlocksLowerTriangular" | custom-call | tf_op jit(solution)/shard_map/triangular_solve/custom-call.0 | solution.py:176
  1184.2 60.9 %all-reduce.22.cloned.1.call-done = f32[1024,256]{0,1:T(8,128)} async-done(((f32[1024,256]{0,1:T(8,128)}), f32[1024,256]{0,1:T(8,128)}) %all-reduce.22.cloned.1.call-update) | async-done | bytes 1048592 | tf_op jit(solution)/shard_map/psum | solution.py:13
  1245.1 10.9 convolution_subtract_fusion
  1265.6 10.7 copy.81
  (190 shorter events, 265.9 us)
Async XLA Ops:
  99.0 77.1 %all-to-all-start = ((bf16[2,2048,768]{2,0,1:T(2,128)(2,1)}), bf16[2,2048,768]{2,0,1:T(2,128)(2,1)}, u32[]{:S(2)}, u32[]{:S(2)}) async-start(bf16[2,2048,768]{2,0,1:T(2,128)(2,1)} %copy.69), calls=%async_computation | async-start | bytes 12582912 | tf_op jit(solution)/shard_map/all_to_all | solution.py:77
  271.0 8.6 copy-start.4
  271.0 300.2 %all-to-all-start.1 = ((bf16[16,2,2048,128]{2,3,1,0:T(8,128)(2,1)}), bf16[16,2,2048,128]{2,3,1,0:T(8,128)(2,1)}, u32[]{:S(2)}, u32[]{:S(2)}) async-start(bf16[16,2,2048,128]{2,3,1,0:T(8,128)(2,1)} %fusion.9), calls=%async_computation.1 | async-start | bytes 33554432 | tf_op jit(solution)/shard_map/all_to_all | solution.py:98
  279.3 436.7 %all-reduce.12.cloned.1.call-start = ((), (), s32[]{:S(2)}) async-start(), calls=%async_computation.2 | async-start | bytes 4194304 | tf_op jit(solution)/shard_map/psum | solution.py:162
  621.3 156.2 %all-reduce.14.cloned.1.call-start = ((), (), s32[]{:S(2)}) async-start(), calls=%async_computation.3 | async-start | bytes 524288 | tf_op jit(solution)/shard_map/psum | solution.py:174
  717.7 207.5 %all-reduce.16.cloned.1.call-start = ((), (), s32[]{:S(2)}) async-start(), calls=%async_computation.4 | async-start | bytes 2097152 | tf_op jit(solution)/shard_map/psum | solution.py:13
  848.4 5.8 copy-start.3
  863.5 167.4 %all-reduce.18.cloned.1.call-start = ((), (), s32[]{:S(2)}) async-start(), calls=%async_computation.5 | async-start | bytes 4194304 | tf_op jit(solution)/shard_map/psum | solution.py:162
  936.0 3.4 copy-start
  941.1 151.2 %all-reduce.20.cloned.1.call-start = ((), (), s32[]{:S(2)}) async-start(), calls=%async_computation.6 | async-start | bytes 524288 | tf_op jit(solution)/shard_map/psum | solution.py:174
  1032.6 212.5 %all-reduce.22.cloned.1.call-start = ((), (), s32[]{:S(2)}) async-start(), calls=%async_computation.7 | async-start | bytes 2097152 | tf_op jit(solution)/shard_map/psum | solution.py:13
  1166.0 5.8 copy-start.2
  1245.1 12.7 copy-start.1
Sparse Core Ops, SparseCore 0:
  621.4 94.5 all-reduce.11
  718.4 58.9 all-reduce.13
  863.7 61.4 all-reduce.15
  941.2 89.7 all-reduce.17
  1033.2 58.9 all-reduce.19
  1183.6 61.4 all-reduce.21
